TPU v7x, 256 devices: a whole 4x4x8 slice. The times are simulated.
256 devices in a mesh: snap: 64 (over x, y, z_hi), feat: 4 (over z_lo, core).
Axes of the slice: x: 4, y: 4, z: 8 (z_hi: 4, z_lo: 2; z = z_hi * 2 + z_lo), core: 2. Of those that a mesh axis runs over, the one named last changes fastest.
Arguments:
- features: bfloat16 [64, 2048, 1024], P('snap', None, 'feat'), may hold values from -6 to 6
- block_index: int32 [64, 16, 8], P('snap'), may hold values from 0 to 15
- block_values: bfloat16 [64, 16, 8, 128, 128], P('snap'), may hold values from -0.1875 to 0.1875
- hop_in: bfloat16 [1024, 1024], P(None, 'feat'), may hold values from -0.1875 to 0.1875
- query_w: bfloat16 [1024, 1024], P(None, 'feat'), may hold values from -0.1875 to 0.1875
- key_w: bfloat16 [1024, 1024], P(None, 'feat'), may hold values from -0.1875 to 0.1875
- value_w: bfloat16 [1024, 1024], P(None, 'feat'), may hold values from -0.1875 to 0.1875
- output_w: bfloat16 [1024, 1024], P(None, 'feat'), may hold values from -0.1875 to 0.1875
- hop_out: bfloat16 [1024, 1024], P(None, 'feat'), may hold values from -0.1875 to 0.1875
- time_bias: float32 [64, 64], replicated, may hold values from -2 to 403
Outputs:
- result: bfloat16 [64, 2048, 1024], P('snap', None, 'feat')
All inputs are finite; a program needn't handle non-finite values.
Results may differ from a plain program's by a relative error of at most 0.012.
Values may be sent and summed in bfloat16 or wider, within the bound.
No kernel may reach another device: no remote copies, remote signals or barrier semaphores. Data moves between devices by JAX's collectives and lax.ppermute only.
A program may use at most 64 MiB of HBM per device.

v0:
```python
import math
import jax
import jax.numpy as jnp
from jax import lax
from jax.sharding import PartitionSpec as P


def sent_to_all(shard, axis):
    copies = jnp.broadcast_to(shard, (lax.axis_size(axis), *shard.shape))
    return lax.all_to_all(copies, axis, split_axis=0, concat_axis=0, tiled=True)


def over_copies(shard, axis):
    everything = sent_to_all(shard, axis)
    return jnp.sum(everything.astype(jnp.float32), axis=0)


def aggregate(field, block_index, block_values):
    count_snap, vertices, columns = field.shape
    rows_blk = block_values.shape[-1]
    blocks = field.reshape(count_snap, vertices // rows_blk, rows_blk, columns)
    picked = jax.vmap(lambda plane, index_row: plane[index_row])(blocks, block_index)
    summed = jnp.einsum(
        "srkij,srkjc->sric", block_values, picked, preferred_element_type=jnp.float32
    )
    return summed.reshape(count_snap, vertices, columns).astype(jnp.bfloat16)


def add_rows(piece, weight):
    return jnp.einsum("svc,cd->svd", piece, weight, preferred_element_type=jnp.float32)


def attend(scores, values, time_bias, score_scale):
    logits = scores * score_scale + time_bias[None]
    shifted = logits - jnp.max(logits, axis=2, keepdims=True)
    weights = jnp.exp(shifted)
    probs = (weights / jnp.sum(weights, axis=2, keepdims=True)).astype(jnp.bfloat16)
    return jnp.einsum("uts,suc->tuc", probs, values, preferred_element_type=jnp.float32).astype(
        jnp.bfloat16
    )


def local(
    features,
    block_index,
    block_values,
    hop_in,
    query_w,
    key_w,
    value_w,
    output_w,
    hop_out,
    time_bias,
):
    score_scale = 1.0 / math.sqrt(query_w.shape[0])
    agg_first = aggregate(features, block_index, block_values)
    lifted = add_rows(lax.all_gather(agg_first, "feat", axis=2, tiled=True), hop_in)
    hidden = jax.nn.relu(lifted).astype(jnp.bfloat16)
    owned_hidden = lax.all_to_all(hidden, "snap", split_axis=1, concat_axis=0, tiled=True)
    piece = lax.all_gather(owned_hidden, "feat", axis=2, tiled=True)
    query_sum = add_rows(piece, query_w)
    keys_sum = add_rows(piece, key_w)
    values_sum = add_rows(piece, value_w)
    query_part = query_sum.astype(jnp.bfloat16)
    keys_part = keys_sum.astype(jnp.bfloat16)
    values_part = values_sum.astype(jnp.bfloat16)
    query_own, keys_own, values_own = (query_part, keys_part, values_part)
    partial_scores = jnp.einsum(
        "tuc,suc->uts", query_own, keys_own, preferred_element_type=jnp.float32
    )
    scores = over_copies(partial_scores.astype(jnp.bfloat16), "feat").astype(jnp.float32)
    context = attend(scores, values_own, time_bias, score_scale)
    gathered = lax.all_to_all(context, "snap", split_axis=0, concat_axis=1, tiled=True)
    update = add_rows(lax.all_gather(gathered, "feat", axis=2, tiled=True), output_w)
    mixed = (hidden.astype(jnp.float32) + update).astype(jnp.bfloat16)
    agg_second = aggregate(mixed, block_index, block_values)
    final_sum = add_rows(lax.all_gather(agg_second, "feat", axis=2, tiled=True), hop_out)
    return jax.nn.relu(final_sum).astype(jnp.bfloat16)


def solution(mesh):
    in_specs = (
        P("snap", None, "feat"),
        P("snap", None, None),
        P("snap", None, None, None, None),
        P(None, "feat"),
        P(None, "feat"),
        P(None, "feat"),
        P(None, "feat"),
        P(None, "feat"),
        P(None, "feat"),
        P(),
    )
    out_specs = P("snap", None, "feat")
    return jax.shard_map(local, mesh=mesh, in_specs=in_specs, out_specs=out_specs, check_vma=False)
```

profile of v0, /device:TPU:1, one launch (start us, length us, event | category | flops | bytes accessed | tf_op | source)
XLA Modules:
  0.0 392.6 jit_solution(9581406341102095699)
XLA Ops:
  6.5 0.0 copy-start
  6.5 0.0 all-gather.5.cloned.1.call-start
  6.5 0.8 fusion.52
  7.3 0.1 copy.21
  7.4 0.1 reshape.87
  7.5 0.3 copy-done
  7.8 6.7 %gather_fusion = bf16[128,128,256]{2,1,0:T(8,128)(2,1)} fusion(bf16[1,16,128,256]{3,2,1,0:T(8,128)(2,1)S(1)} %bitcast.85, s32[128]{0:T(128)S(1)} %reshape.87), kind=kCustom, calls=%fused_computation | custom fusion | bytes 16778240 | tf_op jit(solution)/shard_map/vmap()/gather | solution.py:22
  14.5 0.0 copy-start.4
  14.5 7.2 %bitcast_convert_fusion.1 = bf16[16,256,128]{1,2,0:T(8,128)(2,1)} fusion(bf16[16,8,128,256]{3,2,1,0:T(8,128)(2,1)} %bitcast.88, bf16[1,16,8,128,128]{4,3,2,1,0:T(8,128)(2,1)} %param.12), kind=kOutput, calls=%fused_computation.22 | convolution fusion | flops 1074266112 | bytes 13631488 | tf_op jit(solution)/shard_map/srkij,srkjc->sric/dot_general | solution.py:23
  21.7 0.0 all-gather.5.cloned.1.call-update
  21.7 0.0 all-gather.7.cloned.1.call-start
  21.8 53.4 %all-gather.5.cloned.1.call-done = bf16[1,2048,1024]{2,1,0:T(8,128)(2,1)} async-done(((bf16[1,2048,256]{2,1,0:T(8,128)(2,1)}), bf16[1,2048,1024]{2,1,0:T(8,128)(2,1)}) %all-gather.5.cloned.1.call-update) | async-done | bytes 4194320 | tf_op jit(solution)/shard_map/all_gather | solution.py:57
  75.1 0.0 copy-done.4
  75.1 3.4 fusion.26
  78.6 0.0 copy-start.2
  78.6 11.7 %copy.29 = bf16[1,2048,256]{2,0,1:T(2,128)(2,1)S(1)} copy(bf16[1,2048,256]{2,1,0:T(8,128)(2,1)S(1)} %bitcast.95) | data formatting | bytes 2097152 | tf_op jit(solution)/shard_map/convert_element_type | solution.py:58
  90.3 0.0 copy-done.2
  90.4 0.5 broadcast.44
  90.9 10.6 %reduce = bf16[2048,256]{1,0:T(8,128)(2,1)S(1)} reduce(bf16[2048,1,256]{2,1,0:T(2,128)(2,1)S(1)} %bitcast.90, bf16[]{:T(256)} %broadcast.44), dimensions={1}, to_apply=%bitcast.84.reduce_sub_computation | reduce | bytes 2097154
  101.5 0.3 reshape.110
  101.8 39.5 %all_to_all.29 = bf16[64,2,4096]{2,1,0:T(2,128)(2,1)S(1)} all-to-all(bf16[64,2,4096]{2,1,0:T(2,128)(2,1)S(1)} %reshape.110), channel_id=1, replica_groups=mesh['snap'=64,'feat'=4] {'snap'}, dimensions={0} | all-to-all | bytes 2097152 | tf_op jit(solution)/shard_map/all_to_all | solution.py:59
  141.3 1.0 reshape.111
  142.4 0.2 copy.27
  142.6 1.6 copy.23
  144.1 0.0 copy-start.5
  144.1 0.0 all-gather.7.cloned.1.call-update
  144.2 0.2 all-gather.9.cloned.1.call-start
  144.4 46.8 %all-gather.7.cloned.1.call-done = bf16[64,32,1024]{2,0,1:T(8,128)(2,1)} async-done(((bf16[64,32,256]{2,0,1:T(8,128)(2,1)}), bf16[64,32,1024]{2,0,1:T(8,128)(2,1)}) %all-gather.7.cloned.1.call-update) | async-done | bytes 4194320 | tf_op jit(solution)/shard_map/all_gather | solution.py:60
  191.2 3.6 convolution_convert_fusion
  194.8 0.0 copy-done.5
  194.8 3.9 fusion.42
  198.6 0.5 broadcast_in_dim.5
  199.2 1.7 reshape.112
  200.9 0.0 copy-start.7
  200.9 16.1 %all_to_all.30 = bf16[4,2,65536]{2,1,0:T(2,128)(2,1)} all-to-all(bf16[4,2,65536]{2,1,0:T(2,128)(2,1)S(1)} %reshape.112), channel_id=1, replica_groups=mesh['snap'=64,'feat'=4] {'feat'}, dimensions={0} | all-to-all | bytes 2097152 | tf_op jit(solution)/shard_map/all_to_all | solution.py:10
  217.0 3.1 reshape.113
  220.1 0.4 convert_reduce_fusion
  220.6 0.0 copy-done.7
  220.6 0.6 fusion.60
  221.2 6.0 %fusion.39 = bf16[64,32,256]{2,0,1:T(8,128)(2,1)S(1)} fusion(bf16[64,32,1024]{2,0,1:T(8,128)(2,1)} %all-gather.7.cloned.1.call-done, bf16[1024,256]{1,0:T(8,128)(2,1)} %param.16, f32[32,64]{1,0:T(8,128)S(1)} %fusion.60, f32[32,64,64]{2,1,0:T(8,128)S(1)} %convert_reduce_fusion, f32[64,64]{1,0:T(8,128)S(1)} %copy-done.7), kind=kOutput, calls=%fused_computation.29 | convolution fusion | flops 1142556672 | bytes 6316032 | tf_op jit(solution)/shard_map/uts,suc->tuc/dot_general | solution.py:38
  227.2 0.0 copy-start.3
  227.2 0.6 copy.24
  227.8 41.7 %all_to_all.31 = bf16[64,32,256]{2,1,0:T(8,128)(2,1)} all-to-all(bf16[64,32,256]{2,1,0:T(8,128)(2,1)S(1)} %copy.24), channel_id=1, replica_groups=mesh['snap'=64,'feat'=4] {'snap'}, dimensions={0} | all-to-all | bytes 2097152 | tf_op jit(solution)/shard_map/all_to_all | solution.py:73
  269.5 0.0 all-gather.9.cloned.1.call-update
  269.6 0.3 all-gather.11.cloned.1.call-start
  269.8 44.8 %all-gather.9.cloned.1.call-done = bf16[1,2048,1024]{2,1,0:T(8,128)(2,1)} async-done(((bf16[1,2048,256]{2,1,0:T(8,128)(2,1)}), bf16[1,2048,1024]{2,1,0:T(8,128)(2,1)}) %all-gather.9.cloned.1.call-update) | async-done | bytes 4194320 | tf_op jit(solution)/shard_map/all_gather | solution.py:74
  314.6 0.0 copy-done.3
  314.6 3.6 fusion.20
  318.2 6.7 %gather_fusion.1 = bf16[128,128,256]{2,1,0:T(8,128)(2,1)} fusion(bf16[1,16,128,256]{3,2,1,0:T(8,128)(2,1)S(1)} %bitcast.86, s32[128]{0:T(128)S(1)} %reshape.87), kind=kCustom, calls=%fused_computation.1 | custom fusion | bytes 16778240 | tf_op jit(solution)/shard_map/vmap()/gather | solution.py:22
  324.9 0.0 copy-start.6
  324.9 7.2 %bitcast_convert_fusion = bf16[16,256,128]{1,2,0:T(8,128)(2,1)} fusion(bf16[16,8,128,256]{3,2,1,0:T(8,128)(2,1)} %bitcast.87, bf16[1,16,8,128,128]{4,3,2,1,0:T(8,128)(2,1)} %param.12), kind=kOutput, calls=%fused_computation.21 | convolution fusion | flops 1074266112 | bytes 13631488 | tf_op jit(solution)/shard_map/srkij,srkjc->sric/dot_general | solution.py:23
  332.2 0.0 all-gather.11.cloned.1.call-update
  332.2 0.0 copy-start.1
  332.2 49.5 %all-gather.11.cloned.1.call-done = bf16[1,2048,1024]{2,1,0:T(8,128)(2,1)} async-done(((bf16[1,2048,256]{2,1,0:T(8,128)(2,1)}), bf16[1,2048,1024]{2,1,0:T(8,128)(2,1)}) %all-gather.11.cloned.1.call-update) | async-done | bytes 4194320 | tf_op jit(solution)/shard_map/all_gather | solution.py:77
  381.7 0.0 copy-done.6
  381.7 4.4 %fusion.29 = bf16[1,2048,256]{2,1,0:T(8,128)(2,1)} fusion(bf16[1024,256]{1,0:T(8,128)(2,1)S(1)} %copy-done.6, bf16[1,2048,1024]{2,1,0:T(8,128)(2,1)} %all-gather.11.cloned.1.call-done), kind=kOutput, calls=%fused_computation.20 | convolution fusion | flops 1074790400 | bytes 5767168 | tf_op jit(solution)/shard_map/svc,cd->svd/dot_general | solution.py:30
  386.1 0.0 copy-done.1
  (2 shorter events, 0.0 us)
Async XLA Ops:
  6.5 1.2 copy-start
  6.5 68.6 %all-gather.5.cloned.1.call-start = ((), (), s32[]{:S(2)}) async-start(), calls=%async_computation.3 | async-start | bytes 5242880 | tf_op jit(solution)/shard_map/all_gather | solution.py:57
  14.5 60.7 %copy-start.4 = (bf16[1024,256]{1,0:T(8,128)(2,1)S(1)}, bf16[1024,256]{1,0:T(8,128)(2,1)}, u32[]{:S(2)}) copy-start(bf16[1024,256]{1,0:T(8,128)(2,1)} %param.13) | copy-start | bytes 1572868
  21.7 169.5 %all-gather.7.cloned.1.call-start = ((), (), s32[]{:S(2)}) async-start(), calls=%async_computation.4 | async-start | bytes 5242880 | tf_op jit(solution)/shard_map/all_gather | solution.py:60
  78.6 11.8 %copy-start.2 = (bf16[2048,256]{1,0:T(8,128)(2,1)}, bf16[2048,256]{1,0:T(8,128)(2,1)S(1)}, u32[]{:S(2)}) copy-start(bf16[2048,256]{1,0:T(8,128)(2,1)S(1)} %fusion.26) | copy-start | bytes 3145732
  144.1 50.6 %copy-start.5 = (bf16[1024,256]{1,0:T(8,128)(2,1)S(1)}, bf16[1024,256]{1,0:T(8,128)(2,1)}, u32[]{:S(2)}) copy-start(bf16[1024,256]{1,0:T(8,128)(2,1)} %param.14) | copy-start | bytes 1572868
  144.2 170.5 %all-gather.9.cloned.1.call-start = ((), (), s32[]{:S(2)}) async-start(), calls=%async_computation.5 | async-start | bytes 5242880 | tf_op jit(solution)/shard_map/all_gather | solution.py:74
  200.9 19.6 %copy-start.7 = (f32[64,64]{1,0:T(8,128)S(1)}, f32[64,64]{1,0:T(8,128)}, u32[]{:S(2)}) copy-start(f32[64,64]{1,0:T(8,128)} %param.19) | copy-start | bytes 49156
  227.2 87.4 %copy-start.3 = (bf16[2048,256]{1,0:T(8,128)(2,1)S(1)}, bf16[2048,256]{1,0:T(8,128)(2,1)}, u32[]{:S(2)}) copy-start(bf16[2048,256]{1,0:T(8,128)(2,1)} %copy-done.2) | copy-start | bytes 3145732
  269.6 112.1 %all-gather.11.cloned.1.call-start = ((), (), s32[]{:S(2)}) async-start(), calls=%async_computation.6 | async-start | bytes 5242880 | tf_op jit(solution)/shard_map/all_gather | solution.py:77
  324.9 56.7 %copy-start.6 = (bf16[1024,256]{1,0:T(8,128)(2,1)S(1)}, bf16[1024,256]{1,0:T(8,128)(2,1)}, u32[]{:S(2)}) copy-start(bf16[1024,256]{1,0:T(8,128)(2,1)} %param.18) | copy-start | bytes 1572868
  332.2 53.9 %copy-start.1 = (bf16[1,2048,256]{2,1,0:T(8,128)(2,1)S(1)}, bf16[1,2048,256]{2,1,0:T(8,128)(2,1)}, u32[]{:S(2)}) copy-start(bf16[1,2048,256]{2,1,0:T(8,128)(2,1)} %param.10) | copy-start | bytes 3145732
Sparse Core Ops, SparseCore 0:
  21.8 53.2 all-gather.4
  144.3 46.8 all-gather.6
  269.7 44.8 all-gather.8
  332.3 49.3 all-gather.10
where the time goes:
time: 393 us
  waiting for transfers between devices  195 us (50%)
  blocking collectives  97.3 us (25%)
  matrix products  39.3 us (10%)
  local copies, waits for them, and re-layouts  35.2 us (9%)
  between operations  13.3 us (3%)
  other arithmetic  12.4 us (3%)
    all_gather x1, waiting for transfers between devices, local(): lax.all_gather(agg_first, 'feat', axis=2, tiled=True)  53.4 us
    all_gather x1, waiting for transfers between devices, local(): lax.all_gather(agg_second, 'feat', axis=2, tiled=True)  49.5 us
    all_gather x1, waiting for transfers between devices, local(): piece = lax.all_gather(owned_hidden, 'feat', axis=2, tiled=True)  46.8 us
    all_gather x1, waiting for transfers between devices, local(): lax.all_gather(gathered, 'feat', axis=2, tiled=True)  44.8 us
    all_to_all x1, blocking collectives, local(): lax.all_to_all(context, 'snap', split_axis=0, concat_axis=1, tiled=True)  41.7 us
    all_to_all x1, blocking collectives, local(): lax.all_to_all(hidden, 'snap', split_axis=1, concat_axis=0, tiled=True)  39.5 us
    all_to_all x1, blocking collectives, sent_to_all(): return lax.all_to_all(copies, axis, split_axis=0, concat_axis=0, tiled=True)  16.1 us
    dot_general x4, matrix products, add_rows(): jnp.einsum('svc,cd->svd', piece, weight, preferred_element_type=jnp.float32)  15 us
  transfers between devices with their start and end apart: 4, of which 4 were waited for; matrix products, arithmetic and copies ran while one was open for 0% of the time, Pallas kernels for 0%

commit v1 on v0

--- a/solution.py
+++ b/solution.py
@@ -56,7 +56,9 @@
     agg_first = aggregate(features, block_index, block_values)
     lifted = add_rows(lax.all_gather(agg_first, "feat", axis=2, tiled=True), hop_in)
     hidden = jax.nn.relu(lifted).astype(jnp.bfloat16)
-    owned_hidden = lax.all_to_all(hidden, "snap", split_axis=1, concat_axis=0, tiled=True)
+    shards = jnp.split(hidden, lax.axis_size("snap"), axis=1)
+    incoming = lax.all_to_all(jnp.stack(shards), "snap", 0, 0)
+    owned_hidden = jnp.concatenate(incoming, axis=0)
     piece = lax.all_gather(owned_hidden, "feat", axis=2, tiled=True)
     query_sum = add_rows(piece, query_w)
     keys_sum = add_rows(piece, key_w)

time: 393 us -> 383 us (0.975)
  local copies, waits for them, and re-layouts: 35.2 us -> 23.2 us
  other arithmetic: 12.4 us -> 1.84 us
  matrix products: 39.3 us -> 49.6 us
    convert_element_type x1 -> x0, local copies, waits for them, and re-layouts: 11.7 us -> none  [local(): hidden = jax.nn.relu(lifted).astype(jnp.bfloat16)]
    unnamed x1 -> x0, other arithmetic: 10.6 us -> none
where the time goes in v1:
time: 383 us; the launch traced here: 382 us
  waiting for transfers between devices  194 us (51%)
  blocking collectives  99.5 us (26%)
  matrix products  49.6 us (13%)
  local copies, waits for them, and re-layouts  23.2 us (6%)
  between operations  13.7 us (4%)
    all_gather x1, waiting for transfers between devices, local(): lax.all_gather(agg_first, 'feat', axis=2, tiled=True)  53.4 us
    all_gather x1, waiting for transfers between devices, local(): lax.all_gather(agg_second, 'feat', axis=2, tiled=True)  49.5 us
    all_gather x1, waiting for transfers between devices, local(): piece = lax.all_gather(owned_hidden, 'feat', axis=2, tiled=True)  46.8 us
    all_gather x1, waiting for transfers between devices, local(): lax.all_gather(gathered, 'feat', axis=2, tiled=True)  44.2 us
    all_to_all x1, blocking collectives, local(): lax.all_to_all(context, 'snap', split_axis=0, concat_axis=1, tiled=True)  42.5 us
    all_to_all x1, blocking collectives, local(): incoming = lax.all_to_all(jnp.stack(shards), 'snap', 0, 0)  39.6 us
    dot_general x4, matrix products, add_rows(): jnp.einsum('svc,cd->svd', piece, weight, preferred_element_type=jnp.float32)  18.4 us
    all_to_all x1, blocking collectives, sent_to_all(): return lax.all_to_all(copies, axis, split_axis=0, concat_axis=0, tiled=True)  17.4 us
  transfers between devices with their start and end apart: 4, of which 4 were waited for; matrix products, arithmetic and copies ran while one was open for 0% of the time, Pallas kernels for 0%

profile of v1, /device:TPU:1, one launch (start us, length us, event | category | flops | bytes accessed | tf_op | source)
XLA Modules:
  0.0 382.4 jit_solution(4764038277613881215)
XLA Ops:
  6.5 0.0 copy-start
  6.5 0.0 all-gather.6.cloned.1.call-start
  6.5 0.8 fusion.77
  7.3 0.1 copy.19
  7.4 0.1 reshape.88
  7.5 0.3 copy-done
  7.8 6.7 %gather_fusion = bf16[128,128,256]{2,1,0:T(8,128)(2,1)} fusion(bf16[1,16,128,256]{3,2,1,0:T(8,128)(2,1)S(1)} %bitcast.334, s32[128]{0:T(128)S(1)} %reshape.88), kind=kCustom, calls=%fused_computation | custom fusion | bytes 16778240 | tf_op jit(solution)/shard_map/vmap()/gather | solution.py:22
  14.5 0.0 copy-start.4
  14.5 7.2 %bitcast_convert_fusion.1 = bf16[16,256,128]{1,2,0:T(8,128)(2,1)} fusion(bf16[16,8,128,256]{3,2,1,0:T(8,128)(2,1)} %bitcast.337, bf16[1,16,8,128,128]{4,3,2,1,0:T(8,128)(2,1)} %param.12), kind=kOutput, calls=%fused_computation.28 | convolution fusion | flops 1074266112 | bytes 13631488 | tf_op jit(solution)/shard_map/srkij,srkjc->sric/dot_general | solution.py:23
  21.7 0.0 all-gather.6.cloned.1.call-update
  21.7 0.0 all-gather.12.cloned.1.call-start
  21.8 53.4 %all-gather.6.cloned.1.call-done = bf16[1,2048,1024]{2,1,0:T(8,128)(2,1)} async-done(((bf16[1,2048,256]{2,1,0:T(8,128)(2,1)}), bf16[1,2048,1024]{2,1,0:T(8,128)(2,1)}) %all-gather.6.cloned.1.call-update) | async-done | bytes 4194320 | tf_op jit(solution)/shard_map/all_gather | solution.py:57
  75.1 0.0 copy-done.4
  75.1 3.4 fusion.32
  78.6 0.0 copy-start.2
  78.6 0.0 copy-start.5
  79.3 0.2 copy-done.2
  79.5 39.6 %all_to_all.22 = bf16[64,1,32,256]{3,2,1,0:T(8,128)(2,1)} all-to-all(bf16[64,1,32,256]{3,2,1,0:T(8,128)(2,1)S(1)} %constant_dynamic-update-slice_fusion), channel_id=1, replica_groups=mesh['snap'=64,'feat'=4] {'snap'}, dimensions={0} | all-to-all | bytes 2097152 | tf_op jit(solution)/shard_map/all_to_all | solution.py:60
  119.2 0.0 all-gather.12.cloned.1.call-update
  119.2 0.2 all-gather.8.cloned.1.call-start
  119.4 46.8 %all-gather.12.cloned.1.call-done = bf16[64,1,32,1024]{3,2,1,0:T(8,128)(2,1)} async-done(((bf16[64,1,32,256]{3,2,1,0:T(8,128)(2,1)}), bf16[64,1,32,1024]{3,2,1,0:T(8,128)(2,1)}) %all-gather.12.cloned.1.call-update) | async-done | bytes 4194320 | tf_op jit(solution)/shard_map/all_gather | solution.py:62
  166.3 0.0 copy-done.5
  166.3 0.0 copy-start.6
  166.3 7.0 %fusion.51 = bf16[64,32,256]{2,0,1:T(8,128)(2,1)S(1)} fusion(bf16[64,32,1024]{2,1,0:T(8,128)(2,1)} %bitcast.405, bf16[1024,256]{1,0:T(8,128)(2,1)S(1)} %copy-done.5), kind=kOutput, calls=%fused_computation.32 | convolution fusion | flops 1074266112 | bytes 5767168 | tf_op jit(solution)/shard_map/svc,cd->svd/dot_general | solution.py:30
  173.2 0.0 copy-done.6
  173.2 7.6 %fusion.65 = bf16[32,64,64]{2,1,0:T(8,128)(2,1)} fusion(bf16[64,32,256]{2,0,1:T(8,128)(2,1)S(1)} %fusion.51, bf16[64,32,1024]{2,1,0:T(8,128)(2,1)} %bitcast.406, bf16[1024,256]{1,0:T(8,128)(2,1)S(1)} %copy-done.6), kind=kOutput, calls=%fused_computation.38 | convolution fusion | flops 1141506048 | bytes 6029312 | tf_op jit(solution)/shard_map/tuc,suc->uts/dot_general | solution.py:70
  180.8 1.6 broadcast_in_dim.5
  182.4 2.7 reshape.112
  185.1 0.0 copy-start.8
  185.1 17.4 %all_to_all.23 = bf16[4,2,65536]{2,1,0:T(2,128)(2,1)} all-to-all(bf16[4,2,65536]{2,1,0:T(2,128)(2,1)} %reshape.112), channel_id=1, replica_groups=mesh['snap'=64,'feat'=4] {'feat'}, dimensions={0} | all-to-all | bytes 2097152 | tf_op jit(solution)/shard_map/all_to_all | solution.py:10
  202.5 3.1 reshape.113
  205.6 0.4 convert_reduce_fusion
  206.0 0.0 copy-start.1
  206.0 1.0 copy-done.1
  207.0 0.0 copy-done.8
  207.0 0.6 fusion.85
  207.6 9.1 %fusion.59 = bf16[64,32,256]{2,0,1:T(8,128)(2,1)S(1)} fusion(bf16[64,32,1024]{2,1,0:T(8,128)(2,1)} %bitcast.407, bf16[1024,256]{1,0:T(8,128)(2,1)} %param.16, f32[32,64]{1,0:T(8,128)S(1)} %fusion.85, f32[32,64,64]{2,1,0:T(8,128)} %copy-done.1, f32[64,64]{1,0:T(8,128)S(1)} %copy-done.8), kind=kOutput, calls=%fused_computation.36 | convolution fusion | flops 1142556672 | bytes 6316032 | tf_op jit(solution)/shard_map/uts,suc->tuc/dot_general | solution.py:38
  216.8 0.0 copy-start.3
  216.8 0.6 copy.23
  217.4 42.5 %all_to_all.24 = bf16[64,32,256]{2,1,0:T(8,128)(2,1)} all-to-all(bf16[64,32,256]{2,1,0:T(8,128)(2,1)S(1)} %copy.23), channel_id=1, replica_groups=mesh['snap'=64,'feat'=4] {'snap'}, dimensions={0} | all-to-all | bytes 2097152 | tf_op jit(solution)/shard_map/all_to_all | solution.py:75
  259.9 0.0 all-gather.8.cloned.1.call-update
  259.9 0.3 all-gather.10.cloned.1.call-start
  260.2 44.2 %all-gather.8.cloned.1.call-done = bf16[1,2048,1024]{2,1,0:T(8,128)(2,1)} async-done(((bf16[1,2048,256]{2,1,0:T(8,128)(2,1)}), bf16[1,2048,1024]{2,1,0:T(8,128)(2,1)}) %all-gather.8.cloned.1.call-update) | async-done | bytes 4194320 | tf_op jit(solution)/shard_map/all_gather | solution.py:76
  304.4 0.0 copy-done.3
  304.4 3.6 fusion.26
  308.0 6.7 %gather_fusion.1 = bf16[128,128,256]{2,1,0:T(8,128)(2,1)} fusion(bf16[1,16,128,256]{3,2,1,0:T(8,128)(2,1)S(1)} %bitcast.335, s32[128]{0:T(128)S(1)} %reshape.88), kind=kCustom, calls=%fused_computation.1 | custom fusion | bytes 16778240 | tf_op jit(solution)/shard_map/vmap()/gather | solution.py:22
  314.7 0.0 copy-start.7
  314.7 7.2 %bitcast_convert_fusion = bf16[16,256,128]{1,2,0:T(8,128)(2,1)} fusion(bf16[16,8,128,256]{3,2,1,0:T(8,128)(2,1)} %bitcast.336, bf16[1,16,8,128,128]{4,3,2,1,0:T(8,128)(2,1)} %param.12), kind=kOutput, calls=%fused_computation.27 | convolution fusion | flops 1074266112 | bytes 13631488 | tf_op jit(solution)/shard_map/srkij,srkjc->sric/dot_general | solution.py:23
  321.9 0.0 all-gather.10.cloned.1.call-update
  321.9 49.5 %all-gather.10.cloned.1.call-done = bf16[1,2048,1024]{2,1,0:T(8,128)(2,1)} async-done(((bf16[1,2048,256]{2,1,0:T(8,128)(2,1)}), bf16[1,2048,1024]{2,1,0:T(8,128)(2,1)}) %all-gather.10.cloned.1.call-update) | async-done | bytes 4194320 | tf_op jit(solution)/shard_map/all_gather | solution.py:79
  371.4 0.0 copy-done.7
  371.4 4.4 %fusion.35 = bf16[1,2048,256]{2,1,0:T(8,128)(2,1)} fusion(bf16[1024,256]{1,0:T(8,128)(2,1)S(1)} %copy-done.7, bf16[1,2048,1024]{2,1,0:T(8,128)(2,1)} %all-gather.10.cloned.1.call-done), kind=kOutput, calls=%fused_computation.26 | convolution fusion | flops 1074790400 | bytes 5767168 | tf_op jit(solution)/shard_map/svc,cd->svd/dot_general | solution.py:30
  (66 shorter events, 0.3 us)
Async XLA Ops:
  6.5 1.2 copy-start
  6.5 68.6 %all-gather.6.cloned.1.call-start = ((), (), s32[]{:S(2)}) async-start(), calls=%async_computation.3 | async-start | bytes 5242880 | tf_op jit(solution)/shard_map/all_gather | solution.py:57
  14.5 60.6 %copy-start.4 = (bf16[1024,256]{1,0:T(8,128)(2,1)S(1)}, bf16[1024,256]{1,0:T(8,128)(2,1)}, u32[]{:S(2)}) copy-start(bf16[1024,256]{1,0:T(8,128)(2,1)} %param.13) | copy-start | bytes 1572868
  21.7 144.5 %all-gather.12.cloned.1.call-start = ((), (), s32[]{:S(2)}) async-start(), calls=%async_computation.6 | async-start | bytes 5242880 | tf_op jit(solution)/shard_map/all_gather | solution.py:62
  78.6 1.0 copy-start.2
  78.6 87.7 %copy-start.5 = (bf16[1024,256]{1,0:T(8,128)(2,1)S(1)}, bf16[1024,256]{1,0:T(8,128)(2,1)}, u32[]{:S(2)}) copy-start(bf16[1024,256]{1,0:T(8,128)(2,1)} %param.14) | copy-start | bytes 1572868
  119.2 185.2 %all-gather.8.cloned.1.call-start = ((), (), s32[]{:S(2)}) async-start(), calls=%async_computation.4 | async-start | bytes 5242880 | tf_op jit(solution)/shard_map/all_gather | solution.py:76
  166.3 7.0 %copy-start.6 = (bf16[1024,256]{1,0:T(8,128)(2,1)S(1)}, bf16[1024,256]{1,0:T(8,128)(2,1)}, u32[]{:S(2)}) copy-start(bf16[1024,256]{1,0:T(8,128)(2,1)} %param.15) | copy-start | bytes 1572868
  185.1 21.9 %copy-start.8 = (f32[64,64]{1,0:T(8,128)S(1)}, f32[64,64]{1,0:T(8,128)}, u32[]{:S(2)}) copy-start(f32[64,64]{1,0:T(8,128)} %param.19) | copy-start | bytes 49156
  206.0 1.0 copy-start.1
  216.8 87.6 %copy-start.3 = (bf16[2048,256]{1,0:T(8,128)(2,1)S(1)}, bf16[2048,256]{1,0:T(8,128)(2,1)}, u32[]{:S(2)}) copy-start(bf16[2048,256]{1,0:T(8,128)(2,1)} %copy-done.2) | copy-start | bytes 3145732
  259.9 111.5 %all-gather.10.cloned.1.call-start = ((), (), s32[]{:S(2)}) async-start(), calls=%async_computation.5 | async-start | bytes 5242880 | tf_op jit(solution)/shard_map/all_gather | solution.py:79
  314.7 56.7 %copy-start.7 = (bf16[1024,256]{1,0:T(8,128)(2,1)S(1)}, bf16[1024,256]{1,0:T(8,128)(2,1)}, u32[]{:S(2)}) copy-start(bf16[1024,256]{1,0:T(8,128)(2,1)} %param.18) | copy-start | bytes 1572868
Sparse Core Ops, SparseCore 0:
  21.8 53.2 all-gather.5
  119.3 46.8 all-gather.11
  260.0 44.2 all-gather.7
  322.1 49.3 all-gather.9
